TPU v7x, 32 devices: a whole 2x2x4 slice. The times are simulated.
32 devices in a mesh: group: 2 (over x), dp: 16 (over z, y, core).
Axes of the slice: x: 2, y: 2, z: 4, core: 2. Of those that a mesh axis runs over, the one named last changes fastest.
Arguments:
- tokens: bfloat16 [512, 4096], P(('group', 'dp')), parts along dimension 0, may hold values from -6 to 6
- cotangent: bfloat16 [512, 8192], P('group', 'dp'), parts along dimension 0, may hold values from -0.75 to 0.75
- token_weight: float32 [512], P('group'), parts along dimension 0, may hold values from 0.5 to 1.5
- weight: bfloat16 [4096, 8192], P(None, 'dp'), may hold values from -0.09375 to 0.09375
- moment_one: bfloat16 [4096, 8192], P(None, 'dp'), may hold values from -6 to 6
- moment_two: bfloat16 [4096, 8192], P(None, 'dp'), may hold values from 0.003 to 10
- adjoint: float32 [4096, 8192], P(None, 'dp'), may hold values from -5 to 5
Outputs:
- theta_bar: float32 [8192, 8192], P('group', 'dp'), parts along dimension 0
- token_scores: float32 [512], P(('group', 'dp')), parts along dimension 0
There are 2 independent parts, one for each index of `group`. A program takes and returns all parts, laid end to end along the dimension named above; an argument that names none is the same for every part. Nothing has to cross between parts.
All inputs are finite; a program needn't handle non-finite values.
Results may differ from a plain program's by a relative error of at most 0.0038.
Values may be sent and summed in bfloat16 or wider, within the bound.
A program may use at most 128 MiB of HBM per device.

v0:
```python
import jax
import jax.numpy as jnp
from jax import lax
from jax.sharding import PartitionSpec as P

D = 4096
FW = 8192


def slopes(gate):
    sig = jax.nn.sigmoid(gate)
    slope = sig * (1.0 + gate * (1.0 - sig))
    curve = sig * (1.0 - sig) * (2.0 + gate * (1.0 - 2.0 * sig))
    return (slope, curve)


def contract_rows(rows, other):
    return lax.dot_general(
        rows, other, (((0,), (0,)), ((), ())), preferred_element_type=jnp.float32
    )


def forward_rows(rows, weight, cot_rows, weight_rows):
    gate = jnp.dot(rows, weight, preferred_element_type=jnp.float32)
    slope, curve = slopes(gate)
    scaled = (weight_rows[:, None] * cot_rows.astype(jnp.float32) * slope).astype(jnp.bfloat16)
    return (gate, scaled)


def backward_rows(rows, grad_adj, gate, cot_rows, weight_rows):
    probe = jnp.dot(rows, grad_adj, preferred_element_type=jnp.float32)
    slope, curve = slopes(gate)
    cot_f = cot_rows.astype(jnp.float32)
    bent = (weight_rows[:, None] * cot_f * curve * probe).astype(jnp.bfloat16)
    score = jnp.sum(cot_f * slope * probe, axis=1)
    return (bent, score)


def adjoint_step(grad, moment_one, moment_two, adjoint):
    first = 0.9 * moment_one.astype(jnp.float32) + 0.1 * grad
    second = 0.95 * moment_two.astype(jnp.float32) + 0.05 * grad * grad
    root = jnp.sqrt(second)
    den = root + 1e-08
    upd = first / den
    sq, cross = lax.psum((jnp.sum(upd * upd), jnp.sum(adjoint * upd)), "dp")
    count = D * FW
    rms = jnp.sqrt(sq / count)
    scale = 1.0 / jnp.maximum(1.0, rms)
    bind = jnp.where(rms > 1.0, 1.0 / (rms * rms * rms), 0.0)
    ubar = -0.01 * scale * adjoint + 0.01 * cross * bind / count * upd
    mbar = ubar / den
    vbar = -ubar * first / (den * den) / (2.0 * root)
    return (0.1 * mbar + 0.1 * grad * vbar).astype(jnp.bfloat16)


def shards(tokens, cotangent, token_weight, weight, moment_one, moment_two, adjoint):
    kept_rows = lax.all_gather(tokens, "dp", axis=0, tiled=True)
    gate, scaled = forward_rows(kept_rows, weight, cotangent, token_weight)
    grad = contract_rows(kept_rows, scaled)
    grad_adj = adjoint_step(grad, moment_one, moment_two, adjoint)
    bent, scores = backward_rows(kept_rows, grad_adj, gate, cotangent, token_weight)
    curvature = contract_rows(kept_rows, bent)
    theta_bar = 0.999 * adjoint + curvature
    token_scores = lax.psum_scatter(scores, "dp", scatter_dimension=0, tiled=True)
    return (theta_bar, token_scores)


def solution(mesh):
    in_specs = (
        P(("group", "dp"), None),
        P("group", "dp"),
        P("group"),
        P(None, "dp"),
        P(None, "dp"),
        P(None, "dp"),
        P(None, "dp"),
    )
    out_specs = (P("group", "dp"), P(("group", "dp")))
    return jax.shard_map(shards, mesh=mesh, in_specs=in_specs, out_specs=out_specs, check_vma=False)
```

profile of v0, /device:TPU:0, one launch (start us, length us, event | category | flops | bytes accessed | tf_op | source)
XLA Modules:
  0.0 176.0 jit_solution(10430388128339516694)
XLA Ops:
  7.2 0.0 all-gather.2.cloned.1.call-start
  7.2 0.7 all-gather.2.cloned.1.call-update
  7.9 8.9 %copy.16 = f32[4096,512]{0,1:T(8,128)} copy(f32[4096,512]{1,0:T(8,128)} %param.13) | data formatting | bytes 16777216 | tf_op args[6]
  16.8 0.0 copy-start.3
  16.8 6.4 %copy.17 = bf16[4096,512]{0,1:T(8,128)(2,1)} copy(bf16[4096,512]{1,0:T(8,128)(2,1)} %param.11) | data formatting | bytes 8388608 | tf_op args[4]
  23.2 0.0 copy-start.1
  23.2 0.0 copy-start.2
  23.2 6.5 %copy.18 = bf16[4096,512]{0,1:T(8,128)(2,1)} copy(bf16[4096,512]{1,0:T(8,128)(2,1)} %param.12) | data formatting | bytes 8388608 | tf_op args[5]
  29.7 0.0 copy-done.3
  29.7 0.6 dynamic-slice
  30.9 23.4 %all-gather.2.cloned.1.call-done = bf16[256,4096]{1,0:T(8,128)(2,1)} async-done(((bf16[16,4096]{1,0:T(8,128)(2,1)}), bf16[256,4096]{1,0:T(8,128)(2,1)}) %all-gather.2.cloned.1.call-update) | async-done | bytes 2097168 | tf_op jit(solution)/shard_map/all_gather | solution.py:57
  54.3 4.1 %fusion.30 = f32[256,512]{1,0:T(8,128)S(1)} fusion(bf16[256,4096]{1,0:T(8,128)(2,1)} %all-gather.2.cloned.1.call-done, bf16[4096,512]{1,0:T(8,128)(2,1)} %param.10), kind=kOutput, calls=%fused_computation.40 | convolution fusion | flops 1073741824 | bytes 6815744 | tf_op jit(solution)/shard_map/dot_general | solution.py:24
  58.4 0.0 copy-done.1
  58.4 0.0 copy-done.2
  58.4 0.0 copy-start
  58.4 15.1 %multiply_reduce_fusion.1 = (f32[]{:T(128)}, f32[]{:T(128)}, f32[512,4096]{1,0:T(8,128)}) fusion(bf16[4096,512]{0,1:T(8,128)(2,1)} %copy.18, bf16[4096,512]{0,1:T(8,128)(2,1)} %copy.17, f32[4096,512]{0,1:T(8,128)} %copy.16, bf16[256,4096]{1,0:T(8,128)(2,1)} %all-gather.2.cloned.1.call-done, bf16[256,512]{1,0:T(8,128)(2,1)S(1)} %copy-done.1, ...), kind=kOutput, calls=%fused_computation.8 | convolution fusion | flops 1106640896 | bytes 28050440 | tf_op jit(solution)/shard_map/dot_general | solution.py:18
  73.5 32.1 %all-reduce.1 = (f32[]{:T(128)}, f32[]{:T(128)}) all-reduce(f32[]{:T(128)} %get-tuple-element.7, f32[]{:T(128)} %get-tuple-element.6), channel_id=1, replica_groups=mesh['group'=2,'dp'=16] {'dp'}, use_global_device_ids=true, to_apply=%region_3.0 | all-reduce | flops 2 | bytes 16 | tf_op jit(solution)/shard_map/psum | solution.py:45
  107.1 0.0 copy-done
  107.1 14.8 %fusion.10 = (f32[256]{0:T(256)S(1)}, f32[256,512]{1,0:T(8,128)S(1)}) fusion(bf16[256,512]{1,0:T(8,128)(2,1)S(1)} %copy-done.1, f32[256,512]{1,0:T(8,128)S(1)} %fusion.30, bf16[256,4096]{1,0:T(8,128)(2,1)S(1)} %copy-done, f32[4096,512]{0,1:T(8,128)} %copy.16, bf16[4096,512]{0,1:T(8,128)(2,1)} %copy.17, f32[512,4096]{1,0:T(8,128)} %get-tuple-element.10, ...), kind=kOutput, calls=%fused_computation.22 | convolution fusion | flops 1127612160 | bytes 28574728 | tf_op jit(solution)/shard_map/dot_general | solution.py:31
  121.9 8.2 %bitcast_add_fusion = f32[4096,512]{0,1:T(8,128)} fusion(f32[4096,512]{0,1:T(8,128)} %copy.16, bf16[256,4096]{1,0:T(8,128)(2,1)S(1)} %copy-done, f32[256,512]{1,0:T(8,128)S(1)} %get-tuple-element.12, bf16[256,512]{1,0:T(8,128)(2,1)S(1)} %copy-done.1, f32[256,512]{1,0:T(8,128)S(1)} %fusion.30, f32[256]{0:T(256)S(1)} %copy-done.2), kind=kOutput, calls=%fused_computation.3 | convolution fusion | flops 1079902208 | bytes 20186112 | tf_op jit(solution)/shard_map/dot_general | solution.py:18
  130.1 8.9 %copy.22 = f32[4096,512]{1,0:T(8,128)} copy(f32[4096,512]{0,1:T(8,128)} %bitcast_add_fusion) | data formatting | bytes 16777216
  139.1 29.5 %all-reduce = f32[256]{0:T(256)S(1)} all-reduce(f32[256]{0:T(256)S(1)} %get-tuple-element.11), channel_id=2, replica_groups=mesh['group'=2,'dp'=16] {'dp'}, use_global_device_ids=true, to_apply=%region_5.6.clone | all-reduce | flops 256 | bytes 2048
  168.5 0.6 dynamic-slice.1
Async XLA Ops:
  7.2 47.2 %all-gather.2.cloned.1.call-start = ((), (), s32[]{:S(2)}) async-start(), calls=%async_computation | async-start | bytes 2228224 | tf_op jit(solution)/shard_map/all_gather | solution.py:57
  16.8 12.9 %copy-start.3 = (u32[32]{0:T(128)S(1)}, u32[32]{0:T(128)}, u32[]{:S(2)}) copy-start(u32[32]{0:T(128)} %constant.31) | copy-start | bytes 388
  23.2 35.2 %copy-start.1 = (bf16[256,512]{1,0:T(8,128)(2,1)S(1)}, bf16[256,512]{1,0:T(8,128)(2,1)}, u32[]{:S(2)}) copy-start(bf16[256,512]{1,0:T(8,128)(2,1)} %param.8) | copy-start | bytes 786436
  23.2 35.2 %copy-start.2 = (f32[256]{0:T(256)S(1)}, f32[256]{0:T(256)}, u32[]{:S(2)}) copy-start(f32[256]{0:T(256)} %param.9) | copy-start | bytes 3076
  58.4 48.7 %copy-start = (bf16[256,4096]{1,0:T(8,128)(2,1)S(1)}, bf16[256,4096]{1,0:T(8,128)(2,1)}, u32[]{:S(2)}) copy-start(bf16[256,4096]{1,0:T(8,128)(2,1)} %all-gather.2.cloned.1.call-done) | copy-start | bytes 6291460
Sparse Core Ops, SparseCore 0:
  10.1 44.1 all-gather.1
where the time goes:
time: 177 us; the launch traced here: 176 us
  blocking collectives  61.6 us (35%)
  matrix products  42.2 us (24%)
  local copies, waits for them, and re-layouts  31.9 us (18%)
  waiting for transfers between devices  24.1 us (14%)
  between operations  16.1 us (9%)
    psum x1, blocking collectives, adjoint_step(): sq, cross = lax.psum((jnp.sum(upd * upd), jnp.sum(adjoint * upd)), 'dp')  32.1 us
    unnamed x14, local copies, waits for them, and re-layouts  31.9 us
    unnamed x1, blocking collectives  29.5 us
    all_gather x1, waiting for transfers between devices, shards(): kept_rows = lax.all_gather(tokens, 'dp', axis=0, tiled=True)  23.4 us
    dot_general x2, matrix products, contract_rows(): lax.dot_general(rows, other, (((0,), (0,)), ((), ())), preferred_element_...  23.3 us
    dot_general x1, matrix products, backward_rows(): probe = jnp.dot(rows, grad_adj, preferred_element_type=jnp.float32)  14.8 us
    dot_general x1, matrix products, forward_rows(): gate = jnp.dot(rows, weight, preferred_element_type=jnp.float32)  4.06 us
  transfers between devices with their start and end apart: 1, of which 1 were waited for; matrix products, arithmetic and copies ran while one was open for 13% of the time, Pallas kernels for 0%

commit v1 on v0

v1 whole, which is shorter than its diff:
```python
import functools

import jax
import jax.numpy as jnp
from jax import lax
from jax.experimental import pallas as pl
from jax.experimental.pallas import tpu as pltpu
from jax.sharding import PartitionSpec as P

D = 4096
FW = 8192
COUNT = D * FW
MESH = pl.DeviceIdType.MESH
KB = 256
STRIP = 16


def dot(a, b):
    return jnp.dot(a, b, preferred_element_type=jnp.float32)


def dot_rows(a, b):
    return lax.dot_general(a, b, (((0,), (0,)), ((), ())), preferred_element_type=jnp.float32)


def main_kernel(
    n, wide,
    x_ref, cot_ref, tw_ref, w_hbm, one_hbm, two_hbm, adj_hbm,
    tok_out, bent_out, score_out,
    tok, w, one, two, adj, upd_s, k_s, gate_s, p_s, q_s, scaled_s, probe_s,
    mine, sums, sc, scs,
    load_sem, own_sem, out_sem, gs, gr, ss, sr, cs, cr,
):
    me = lax.axis_index("dp")
    line = n // (2 * wide)
    core = lax.rem(me, 2)
    y = lax.rem(me // 2, wide)
    z = me // (2 * wide)
    stride = 2 * wide
    sibling = me + 1 - 2 * core
    across = me + (1 - 2 * y) * 2
    rows = x_ref.shape[0]
    tokens, width = scaled_s.shape

    loads = [
        pltpu.make_async_copy(src, dst, load_sem.at[i])
        for i, (src, dst) in enumerate(
            ((w_hbm, w), (two_hbm, two), (one_hbm, one), (adj_hbm, adj)))
    ]

    def slab(o):
        return tok.at[pl.ds(pl.multiple_of(o * rows, rows), rows), :]

    own = pltpu.make_async_copy(x_ref, slab(me), own_sem)

    barrier = pltpu.get_barrier_semaphore()

    def greet(k, _):
        pl.semaphore_signal(barrier, inc=1, device_id={"dp": lax.rem(me + k, n)}, device_id_type=MESH)
        return 0

    lax.fori_loop(1, n, greet, 0)
    for copy in loads:
        copy.start()
    own.start()
    pl.semaphore_wait(barrier, n - 1)

    def push(kind, o, dev, src=None):
        return pltpu.make_async_remote_copy(
            src_ref=slab(o) if src is None else src,
            dst_ref=slab(o),
            send_sem=gs.at[kind, o],
            recv_sem=gr.at[o],
            device_id={"dp": dev},
            device_id_type=MESH,
        )

    def arrive(o):
        push(3, o, sibling).wait_recv()

    more, less = z + 1 < line, z > 0

    @pl.when(more)
    def _():
        push(0, me, me + stride, x_ref).start()

    @pl.when(less)
    def _():
        push(1, me, me - stride, x_ref).start()

    if wide == 2:
        push(2, me, across, x_ref).start()
    push(3, me, sibling, x_ref).start()

    def from_across(k):
        if wide != 2:
            return
        for way in (-1, 1) if k else (1,):
            o = across + way * k * stride

            @pl.when((z + way * k >= 0) & (z + way * k < line))
            def _():
                arrive(o)
                push(3, o, sibling).start()

    for k in range(1, line):
        for way, kind, onward in ((-1, 0, more), (1, 1, less)):
            o = me + way * k * stride

            @pl.when((z + way * k >= 0) & (z + way * k < line))
            def _():
                arrive(o)

                @pl.when(onward)
                def _():
                    push(kind, o, me - way * stride).start()

                if wide == 2:
                    push(2, o, across).start()
                push(3, o, sibling).start()

        from_across(k - 1)
    from_across(line - 1)

    def from_sibling(i, _):
        arrive(2 * i + 1 - core)
        return 0

    lax.fori_loop(0, n // 2, from_sibling, 0)
    own.wait()
    keep = pltpu.make_async_copy(tok, tok_out, out_sem)
    keep.start()

    loads[0].wait()
    gate_s[...] = jnp.zeros_like(gate_s)

    def gate_step(i, _):
        ks = pl.ds(pl.multiple_of(i * 512, 512), 512)
        gate_s[...] += dot(tok[:, ks], w[ks, :])
        return 0

    lax.fori_loop(0, D // 512, gate_step, 0)

    tw = jnp.transpose(jnp.broadcast_to(tw_ref[...], (128, tokens)))
    q_s[:, 0:128] = tw

    def slope_step(i, _):
        rs = pl.ds(pl.multiple_of(i * STRIP, STRIP), STRIP)
        tw = q_s[rs, 0:128]
        for j in range(width // 128):
            js = slice(j * 128, (j + 1) * 128)
            gate = gate_s[rs, js]
            cot = cot_ref[rs, js].astype(jnp.float32)
            sig = jax.nn.sigmoid(gate)
            slope = sig * (1.0 + gate * (1.0 - sig))
            curve = sig * (1.0 - sig) * (2.0 + gate * (1.0 - 2.0 * sig))
            scaled_s[rs, js] = (tw * cot * slope).astype(jnp.bfloat16)
            p_s[rs, js] = cot * slope
            q_s[rs, js] = tw * cot * curve
        return 0

    lax.fori_loop(0, tokens // STRIP, slope_step, 0, unroll=4)

    for copy in loads[1:]:
        copy.wait()

    def fold(v):
        out = None
        for i in range(v.shape[0] // 8):
            for j in range(width // 128):
                part = v[i * 8:(i + 1) * 8, j * 128:(j + 1) * 128]
                out = part if out is None else out + part
        return out

    def grad_step(i, carry):
        sq, cross = carry
        base = pl.multiple_of(i * KB, KB)
        g_all = dot_rows(tok[:, pl.ds(base, KB)], scaled_s[...])
        for r in range(0, KB, STRIP):
            rs = pl.ds(pl.multiple_of(base + r, STRIP), STRIP)
            g = g_all[r:r + STRIP]
            first = 0.9 * one[rs, :].astype(jnp.float32) + 0.1 * g
            second = 0.95 * two[rs, :].astype(jnp.float32) + 0.05 * g * g
            inv_root = lax.rsqrt(second)
            den = second * inv_root + 1e-08
            inv = lax.rsqrt(den * den)
            upd = first * inv
            upd_s[rs, :] = upd
            k_s[rs, :] = (0.1 * inv) * (1.0 - 0.5 * (g * upd) * inv_root)
            sq = sq + fold(upd * upd)
            cross = cross + fold(adj[rs, :] * upd)
        return sq, cross

    zero = jnp.zeros((8, 128), jnp.float32)
    sq, cross = lax.fori_loop(0, D // KB, grad_step, (zero, zero))
    mine[0] = sq
    mine[1] = cross
    sums[me, 0] = sq
    sums[me, 1] = cross

    def sum_copy(k):
        return pltpu.make_async_remote_copy(
            src_ref=mine, dst_ref=sums.at[me],
            send_sem=ss.at[k], recv_sem=sr.at[me],
            device_id={"dp": lax.rem(me + k, n)}, device_id_type=MESH)

    def sum_arrive(k):
        o = lax.rem(me + k, n)
        pltpu.make_async_remote_copy(
            src_ref=mine, dst_ref=sums.at[o],
            send_sem=ss.at[k], recv_sem=sr.at[o],
            device_id={"dp": o}, device_id_type=MESH).wait_recv()

    def each(body):
        def step(k, _):
            body(k)
            return 0

        lax.fori_loop(1, n, step, 0)

    each(lambda k: sum_copy(k).start())
    probe_s[...] = jnp.zeros_like(probe_s)
    each(sum_arrive)

    tot = sums[0]
    for o in range(1, n):
        tot = tot + sums[o]
    sq = jnp.sum(tot[0], keepdims=True)
    cross = jnp.sum(tot[1], keepdims=True)
    rms = jnp.sqrt(sq / COUNT)
    scale = 1.0 / jnp.maximum(1.0, rms)
    bind = jnp.where(rms > 1.0, 1.0 / (rms * rms * rms), 0.0)
    alpha = jnp.broadcast_to(-0.01 * scale, (STRIP, width))
    beta = jnp.broadcast_to(0.01 * cross * bind / COUNT, (STRIP, width))

    def probe_step(i, _):
        base = pl.multiple_of(i * 512, 512)
        parts = []
        for r in range(0, 512, STRIP):
            rs = pl.ds(pl.multiple_of(base + r, STRIP), STRIP)
            ubar = alpha * adj[rs, :] + beta * upd_s[rs, :]
            parts.append((ubar * k_s[rs, :]).astype(jnp.bfloat16))
        probe_s[...] += dot(tok[:, pl.ds(base, 512)], jnp.concatenate(parts, axis=0))
        return 0

    lax.fori_loop(0, D // 512, probe_step, 0)

    def score_step(i, _):
        rs = pl.ds(pl.multiple_of(i * STRIP, STRIP), STRIP)
        out = None
        for j in range(width // 128):
            js = slice(j * 128, (j + 1) * 128)
            part = p_s[rs, js] * probe_s[rs, js]
            out = part if out is None else out + part
        sc[rs, :] = out
        return 0

    lax.fori_loop(0, tokens // STRIP, score_step, 0, unroll=4)

    def sc_rows(o):
        return sc.at[pl.ds(pl.multiple_of(o * rows, rows), rows), :]

    scs[me] = sc[pl.ds(pl.multiple_of(me * rows, rows), rows), :]

    def score_copy(k):
        o = lax.rem(me + k, n)
        return pltpu.make_async_remote_copy(
            src_ref=sc_rows(o), dst_ref=scs.at[me],
            send_sem=cs.at[k], recv_sem=cr.at[me],
            device_id={"dp": o}, device_id_type=MESH)

    def score_arrive(k):
        o = lax.rem(me + k, n)
        pltpu.make_async_remote_copy(
            src_ref=sc_rows(o), dst_ref=scs.at[o],
            send_sem=cs.at[k], recv_sem=cr.at[o],
            device_id={"dp": o}, device_id_type=MESH).wait_recv()

    each(lambda k: score_copy(k).start())

    def bent_step(i, _):
        rs = pl.ds(pl.multiple_of(i * STRIP, STRIP), STRIP)
        bent_out[rs, :] = (q_s[rs, :] * probe_s[rs, :]).astype(jnp.bfloat16)
        return 0

    lax.fori_loop(0, tokens // STRIP, bent_step, 0, unroll=4)

    def sent_line(i, _):
        o = (i * wide + y) * 2 + core

        @pl.when((i <= z) & more)
        def _():
            push(0, o, me + stride).wait_send()

        @pl.when((i >= z) & less)
        def _():
            push(1, o, me - stride).wait_send()

        if wide == 2:
            push(2, o, across).wait_send()
        return 0

    lax.fori_loop(0, line, sent_line, 0)

    def sent_core(i, _):
        push(3, 2 * i + core, sibling).wait_send()
        return 0

    lax.fori_loop(0, n // 2, sent_core, 0)
    each(lambda k: sum_copy(k).wait_send())
    each(score_arrive)
    tot = scs[0]
    for o in range(1, n):
        tot = tot + scs[o]
    score_out[...] = tot
    each(lambda k: score_copy(k).wait_send())
    keep.wait()


def last_kernel(tok_ref, bent_ref, adj_ref, sc_ref, theta_ref, score_ref):
    theta_ref[...] = 0.999 * adj_ref[...] + dot_rows(tok_ref[...], bent_ref[...])

    @pl.when(pl.program_id(0) == 0)
    def _():
        rows = sc_ref.shape[0]
        total = jnp.sum(sc_ref[...], axis=1, keepdims=True)
        at = lax.broadcasted_iota(jnp.int32, (rows, 128), 0)
        lane = lax.broadcasted_iota(jnp.int32, (rows, 128), 1)
        row = jnp.sum(jnp.where(at == lane, total, 0.0), axis=0, keepdims=True)
        score_ref[...] = row[:, :rows]


def shards(n, wide, x, cotangent, token_weight, weight, moment_one, moment_two, adjoint):
    rows = x.shape[0]
    tokens = n * rows
    width = weight.shape[1]
    f32, bf16 = jnp.float32, jnp.bfloat16
    vm = pl.BlockSpec(memory_space=pltpu.VMEM)
    hbm = pl.BlockSpec(memory_space=pl.ANY)
    dma = pltpu.SemaphoreType.DMA
    tok, bent, sc = pl.pallas_call(
        functools.partial(main_kernel, n, wide),
        out_shape=(
            jax.ShapeDtypeStruct((tokens, D), bf16),
            jax.ShapeDtypeStruct((tokens, width), bf16),
            jax.ShapeDtypeStruct((rows, 128), f32),
        ),
        in_specs=[hbm, vm, vm, hbm, hbm, hbm, hbm],
        out_specs=(hbm, vm, vm),
        scratch_shapes=[
            pltpu.VMEM((tokens, D), bf16),
            pltpu.VMEM((D, width), bf16),
            pltpu.VMEM((D, width), bf16),
            pltpu.VMEM((D, width), bf16),
            pltpu.VMEM((D, width), f32),
            pltpu.VMEM((D, width), f32),
            pltpu.VMEM((D, width), f32),
            pltpu.VMEM((tokens, width), f32),
            pltpu.VMEM((tokens, width), f32),
            pltpu.VMEM((tokens, width), f32),
            pltpu.VMEM((tokens, width), bf16),
            pltpu.VMEM((tokens, width), f32),
            pltpu.VMEM((2, 8, 128), f32),
            pltpu.VMEM((n, 2, 8, 128), f32),
            pltpu.VMEM((tokens, 128), f32),
            pltpu.VMEM((n, rows, 128), f32),
            dma((4,)),
            dma,
            dma,
            dma((4, n)),
            dma((n,)),
            dma((n,)),
            dma((n,)),
            dma((n,)),
            dma((n,)),
        ],
        compiler_params=pltpu.CompilerParams(
            collective_id=0, has_side_effects=True, vmem_limit_bytes=60 * 2**20
        ),
    )(x, cotangent, token_weight.reshape(1, tokens), weight, moment_one, moment_two, adjoint)
    step = 512
    theta, score = pl.pallas_call(
        last_kernel,
        grid=(D // step,),
        out_shape=(
            jax.ShapeDtypeStruct((D, width), f32),
            jax.ShapeDtypeStruct((1, rows), f32),
        ),
        in_specs=[
            pl.BlockSpec((tokens, step), lambda i: (0, i)),
            pl.BlockSpec((tokens, width), lambda i: (0, 0)),
            pl.BlockSpec((step, width), lambda i: (i, 0)),
            pl.BlockSpec((rows, 128), lambda i: (0, 0)),
        ],
        out_specs=(
            pl.BlockSpec((step, width), lambda i: (i, 0)),
            pl.BlockSpec((1, rows), lambda i: (0, 0)),
        ),
    )(tok, bent, adjoint, sc)
    return theta, score.reshape(rows)


def solution(mesh):
    n = mesh.shape["dp"]
    wide = 2 if mesh.shape["group"] == 2 else 1
    in_specs = (
        P(("group", "dp"), None),
        P("group", "dp"),
        P("group"),
        P(None, "dp"),
        P(None, "dp"),
        P(None, "dp"),
        P(None, "dp"),
    )
    out_specs = (P("group", "dp"), P(("group", "dp")))
    return jax.shard_map(
        functools.partial(shards, n, wide), mesh=mesh,
        in_specs=in_specs, out_specs=out_specs, check_vma=False)
```

time: 177 us -> 63.1 us (0.36)
  Pallas kernels: 0 us -> 62.1 us
  blocking collectives: 61.6 us -> 0 us
  matrix products: 42.2 us -> 0 us
  local copies, waits for them, and re-layouts: 31.9 us -> 0 us
  waiting for transfers between devices: 24.1 us -> 0 us
  between operations: 16.1 us -> 0.64 us
    pallas_call x0 -> x2, Pallas kernels: none -> 62.1 us  [the longest x1 51.7 us: shards(): pl.pallas_call(functools.partial(main_kernel, n, wide), out_shape=(jax.Sh...]
    dot_general x4 -> x0, matrix products: 42.2 us -> none  [the longest x2 23.3 us: contract_rows(): lax.dot_general(rows, other, (((0,), (0,)), ((), ())), preferred_element_...]
    psum x1 -> x0, blocking collectives: 32.1 us -> none  [adjoint_step(): sq, cross = lax.psum((jnp.sum(upd * upd), jnp.sum(adjoint * upd)), 'dp')]
    unnamed x14 -> x0, local copies, waits for them, and re-layouts: 31.9 us -> none
    unnamed x1 -> x0, blocking collectives: 29.5 us -> none
    all_gather x1 -> x0, waiting for transfers between devices: 23.4 us -> none  [shards(): kept_rows = lax.all_gather(tokens, 'dp', axis=0, tiled=True)]
  transfers between devices with their start and end apart: 1 -> 0, of which waited for: 1 -> 0; matrix products, arithmetic and copies ran while one was open for 13% -> 0% of each run, Pallas kernels for 0% -> 0%
where the time goes in v1:
time: 63.1 us; the launch traced here: 62.7 us
  Pallas kernels  62.1 us (98%)
  between operations  0.64 us (1%)
    pallas_call x1, Pallas kernels, shards(): pl.pallas_call(functools.partial(main_kernel, n, wide), out_shape=(jax.Sh...  51.7 us
    pallas_call x1, Pallas kernels, shards(): pl.pallas_call(last_kernel, grid=(D // step,), out_shape=(jax.ShapeDtypeS...  10.4 us

profile of v1, /device:TPU:0, one launch (start us, length us, event | category | flops | bytes accessed | tf_op | source)
XLA Modules:
  0.0 62.7 jit_solution(8340944255548982185)
XLA Ops:
  0.6 51.7 %shard_map.86 = (bf16[256,4096]{1,0:T(8,128)(2,1)}, bf16[256,512]{1,0:T(8,128)(2,1)}, f32[16,128]{1,0:T(8,128)}) custom-call(bf16[16,4096]{1,0:T(8,128)(2,1)} %x_ref.1, bf16[256,512]{1,0:T(8,128)(2,1)} %cot_ref.1, f32[1,256]{1,0:T(1,128)} %bitcast.2, bf16[4096,512]{1,0:T(8,128)(2,1)} %w_hbm.1, bf16[4096,512]{1,0:T(8,128)(2,1)} %one_hbm.1, ...), custom_call_target="tpu_custom_call" | custom-call | tf_op jit(solution)/shard_map/pallas_call | solution.py:341
  52.3 10.4 %shard_map.87 = (f32[4096,512]{1,0:T(8,128)}, f32[1,16]{1,0:T(1,128)}) custom-call(bf16[256,4096]{1,0:T(8,128)(2,1)} %get-tuple-element.7.tok_ref, bf16[256,512]{1,0:T(8,128)(2,1)} %get-tuple-element.8.bent_ref, f32[4096,512]{1,0:T(8,128)} %adj_ref.1, f32[16,128]{1,0:T(8,128)} %get-tuple-element.9.sc_ref), custom_call_target="tpu_custom_call" | custom-call | tf_op jit(solution)/shard_map/pallas_call | solution.py:382

commit v2 on v1

--- a/solution.py
+++ b/solution.py
@@ -13,6 +13,8 @@
 MESH = pl.DeviceIdType.MESH
 KB = 256
 STRIP = 16
+PIECES = 1
+LAST = 8
 
 
 def dot(a, b):
@@ -48,10 +50,12 @@
             ((w_hbm, w), (two_hbm, two), (one_hbm, one), (adj_hbm, adj)))
     ]
 
-    def slab(o):
-        return tok.at[pl.ds(pl.multiple_of(o * rows, rows), rows), :]
-
-    own = pltpu.make_async_copy(x_ref, slab(me), own_sem)
+    cols = D // PIECES
+
+    def slab(o, h):
+        return tok.at[pl.ds(pl.multiple_of(o * rows, rows), rows), pl.ds(h * cols, cols)]
+
+    own = pltpu.make_async_copy(x_ref, tok.at[pl.ds(pl.multiple_of(me * rows, rows), rows), :], own_sem)
 
     barrier = pltpu.get_barrier_semaphore()
 
@@ -65,34 +69,35 @@
     own.start()
     pl.semaphore_wait(barrier, n - 1)
 
-    def push(kind, o, dev, src=None):
+    def push(kind, o, dev, h, src=None):
         return pltpu.make_async_remote_copy(
-            src_ref=slab(o) if src is None else src,
-            dst_ref=slab(o),
-            send_sem=gs.at[kind, o],
-            recv_sem=gr.at[o],
+            src_ref=slab(o, h) if src is None else src.at[:, pl.ds(h * cols, cols)],
+            dst_ref=slab(o, h),
+            send_sem=gs.at[kind, h, o],
+            recv_sem=gr.at[h, o],
             device_id={"dp": dev},
             device_id_type=MESH,
         )
 
-    def arrive(o):
-        push(3, o, sibling).wait_recv()
+    def arrive(o, h):
+        push(3, o, sibling, h).wait_recv()
 
     more, less = z + 1 < line, z > 0
 
-    @pl.when(more)
-    def _():
-        push(0, me, me + stride, x_ref).start()
-
-    @pl.when(less)
-    def _():
-        push(1, me, me - stride, x_ref).start()
-
-    if wide == 2:
-        push(2, me, across, x_ref).start()
-    push(3, me, sibling, x_ref).start()
-
-    def from_across(k):
+    for h in range(PIECES):
+        @pl.when(more)
+        def _():
+            push(0, me, me + stride, h, x_ref).start()
+
+        @pl.when(less)
+        def _():
+            push(1, me, me - stride, h, x_ref).start()
+
+        if wide == 2:
+            push(2, me, across, h, x_ref).start()
+        push(3, me, sibling, h, x_ref).start()
+
+    def from_across(k, h):
         if wide != 2:
             return
         for way in (-1, 1) if k else (1,):
@@ -100,30 +105,33 @@
 
             @pl.when((z + way * k >= 0) & (z + way * k < line))
             def _():
-                arrive(o)
-                push(3, o, sibling).start()
+                arrive(o, h)
+                push(3, o, sibling, h).start()
 
     for k in range(1, line):
-        for way, kind, onward in ((-1, 0, more), (1, 1, less)):
-            o = me + way * k * stride
-
-            @pl.when((z + way * k >= 0) & (z + way * k < line))
-            def _():
-                arrive(o)
-
-                @pl.when(onward)
+        for h in range(PIECES):
+            for way, kind, onward in ((-1, 0, more), (1, 1, less)):
+                o = me + way * k * stride
+
+                @pl.when((z + way * k >= 0) & (z + way * k < line))
                 def _():
-                    push(kind, o, me - way * stride).start()
-
-                if wide == 2:
-                    push(2, o, across).start()
-                push(3, o, sibling).start()
-
-        from_across(k - 1)
-    from_across(line - 1)
+                    arrive(o, h)
+
+                    @pl.when(onward)
+                    def _():
+                        push(kind, o, me - way * stride, h).start()
+
+                    if wide == 2:
+                        push(2, o, across, h).start()
+                    push(3, o, sibling, h).start()
+
+            from_across(k - 1, h)
+    for h in range(PIECES):
+        from_across(line - 1, h)
 
     def from_sibling(i, _):
-        arrive(2 * i + 1 - core)
+        for h in range(PIECES):
+            arrive(2 * i + 1 - core, h)
         return 0
 
     lax.fori_loop(0, n // 2, from_sibling, 0)
@@ -193,10 +201,10 @@
 
     zero = jnp.zeros((8, 128), jnp.float32)
     sq, cross = lax.fori_loop(0, D // KB, grad_step, (zero, zero))
-    mine[0] = sq
-    mine[1] = cross
-    sums[me, 0] = sq
-    sums[me, 1] = cross
+    pair = jnp.concatenate(
+        [jnp.sum(sq, axis=0, keepdims=True), jnp.sum(cross, axis=0, keepdims=True)], axis=0)
+    mine[...] = pair
+    sums[me] = pair
 
     def sum_copy(k):
         return pltpu.make_async_remote_copy(
@@ -225,8 +233,8 @@
     tot = sums[0]
     for o in range(1, n):
         tot = tot + sums[o]
-    sq = jnp.sum(tot[0], keepdims=True)
-    cross = jnp.sum(tot[1], keepdims=True)
+    sq = jnp.sum(tot[0:1], keepdims=True)
+    cross = jnp.sum(tot[1:2], keepdims=True)
     rms = jnp.sqrt(sq / COUNT)
     scale = 1.0 / jnp.maximum(1.0, rms)
     bind = jnp.where(rms > 1.0, 1.0 / (rms * rms * rms), 0.0)
@@ -245,22 +253,26 @@
 
     lax.fori_loop(0, D // 512, probe_step, 0)
 
+    at = lax.broadcasted_iota(jnp.int32, (rows, 128), 0)
+    lane = lax.broadcasted_iota(jnp.int32, (rows, 128), 1)
+
     def score_step(i, _):
-        rs = pl.ds(pl.multiple_of(i * STRIP, STRIP), STRIP)
+        rs = pl.ds(pl.multiple_of(i * rows, rows), rows)
         out = None
         for j in range(width // 128):
             js = slice(j * 128, (j + 1) * 128)
             part = p_s[rs, js] * probe_s[rs, js]
             out = part if out is None else out + part
-        sc[rs, :] = out
-        return 0
-
-    lax.fori_loop(0, tokens // STRIP, score_step, 0, unroll=4)
+        total = jnp.sum(out, axis=1, keepdims=True)
+        sc[i] = jnp.sum(jnp.where(at == lane, total, 0.0), axis=0, keepdims=True)
+        return 0
+
+    lax.fori_loop(0, n, score_step, 0, unroll=4)
 
     def sc_rows(o):
-        return sc.at[pl.ds(pl.multiple_of(o * rows, rows), rows), :]
-
-    scs[me] = sc[pl.ds(pl.multiple_of(me * rows, rows), rows), :]
+        return sc.at[o]
+
+    scs[me] = sc[me]
 
     def score_copy(k):
         o = lax.rem(me + k, n)
@@ -287,23 +299,24 @@
 
     def sent_line(i, _):
         o = (i * wide + y) * 2 + core
-
-        @pl.when((i <= z) & more)
-        def _():
-            push(0, o, me + stride).wait_send()
-
-        @pl.when((i >= z) & less)
-        def _():
-            push(1, o, me - stride).wait_send()
-
-        if wide == 2:
-            push(2, o, across).wait_send()
+        for h in range(PIECES):
+            @pl.when((i <= z) & more)
+            def _():
+                push(0, o, me + stride, h).wait_send()
+
+            @pl.when((i >= z) & less)
+            def _():
+                push(1, o, me - stride, h).wait_send()
+
+            if wide == 2:
+                push(2, o, across, h).wait_send()
         return 0
 
     lax.fori_loop(0, line, sent_line, 0)
 
     def sent_core(i, _):
-        push(3, 2 * i + core, sibling).wait_send()
+        for h in range(PIECES):
+            push(3, 2 * i + core, sibling, h).wait_send()
         return 0
 
     lax.fori_loop(0, n // 2, sent_core, 0)
@@ -317,17 +330,25 @@
     keep.wait()
 
 
-def last_kernel(tok_ref, bent_ref, adj_ref, sc_ref, theta_ref, score_ref):
-    theta_ref[...] = 0.999 * adj_ref[...] + dot_rows(tok_ref[...], bent_ref[...])
-
-    @pl.when(pl.program_id(0) == 0)
-    def _():
-        rows = sc_ref.shape[0]
-        total = jnp.sum(sc_ref[...], axis=1, keepdims=True)
-        at = lax.broadcasted_iota(jnp.int32, (rows, 128), 0)
-        lane = lax.broadcasted_iota(jnp.int32, (rows, 128), 1)
-        row = jnp.sum(jnp.where(at == lane, total, 0.0), axis=0, keepdims=True)
-        score_ref[...] = row[:, :rows]
+def last_kernel(tok_hbm, bent_ref, adj_hbm, sc_ref, theta_hbm, score_ref, tok, adj, theta, tok_sem, adj_sem, out_sem):
+    step = D // LAST
+    parts = [pl.ds(i * step, step) for i in range(LAST)]
+    toks = [pltpu.make_async_copy(tok_hbm.at[:, p], tok.at[:, p], tok_sem.at[i]) for i, p in enumerate(parts)]
+    adjs = [pltpu.make_async_copy(adj_hbm.at[p, :], adj.at[p, :], adj_sem.at[i]) for i, p in enumerate(parts)]
+    outs = [pltpu.make_async_copy(theta.at[p, :], theta_hbm.at[p, :], out_sem.at[i]) for i, p in enumerate(parts)]
+    for i in range(LAST):
+        toks[i].start()
+        adjs[i].start()
+
+    score_ref[...] = sc_ref[:, :score_ref.shape[1]]
+
+    for i, p in enumerate(parts):
+        toks[i].wait()
+        adjs[i].wait()
+        theta[p, :] = 0.999 * adj[p, :] + dot_rows(tok[:, p], bent_ref[...])
+        outs[i].start()
+    for copy in outs:
+        copy.wait()
 
 
 def shards(n, wide, x, cotangent, token_weight, weight, moment_one, moment_two, adjoint):
@@ -343,7 +364,7 @@
         out_shape=(
             jax.ShapeDtypeStruct((tokens, D), bf16),
             jax.ShapeDtypeStruct((tokens, width), bf16),
-            jax.ShapeDtypeStruct((rows, 128), f32),
+            jax.ShapeDtypeStruct((1, 128), f32),
         ),
         in_specs=[hbm, vm, vm, hbm, hbm, hbm, hbm],
         out_specs=(hbm, vm, vm),
@@ -360,15 +381,15 @@
             pltpu.VMEM((tokens, width), f32),
             pltpu.VMEM((tokens, width), bf16),
             pltpu.VMEM((tokens, width), f32),
-            pltpu.VMEM((2, 8, 128), f32),
-            pltpu.VMEM((n, 2, 8, 128), f32),
-            pltpu.VMEM((tokens, 128), f32),
-            pltpu.VMEM((n, rows, 128), f32),
+            pltpu.VMEM((2, 128), f32),
+            pltpu.VMEM((n, 2, 128), f32),
+            pltpu.VMEM((n, 1, 128), f32),
+            pltpu.VMEM((n, 1, 128), f32),
             dma((4,)),
             dma,
             dma,
-            dma((4, n)),
-            dma((n,)),
+            dma((4, PIECES, n)),
+            dma((PIECES, n)),
             dma((n,)),
             dma((n,)),
             dma((n,)),
@@ -378,24 +399,23 @@
             collective_id=0, has_side_effects=True, vmem_limit_bytes=60 * 2**20
         ),
     )(x, cotangent, token_weight.reshape(1, tokens), weight, moment_one, moment_two, adjoint)
-    step = 512
     theta, score = pl.pallas_call(
         last_kernel,
-        grid=(D // step,),
         out_shape=(
             jax.ShapeDtypeStruct((D, width), f32),
             jax.ShapeDtypeStruct((1, rows), f32),
         ),
-        in_specs=[
-            pl.BlockSpec((tokens, step), lambda i: (0, i)),
-            pl.BlockSpec((tokens, width), lambda i: (0, 0)),
-            pl.BlockSpec((step, width), lambda i: (i, 0)),
-            pl.BlockSpec((rows, 128), lambda i: (0, 0)),
+        in_specs=[hbm, vm, hbm, vm],
+        out_specs=(hbm, vm),
+        scratch_shapes=[
+            pltpu.VMEM((tokens, D), bf16),
+            pltpu.VMEM((D, width), f32),
+            pltpu.VMEM((D, width), f32),
+            dma((LAST,)),
+            dma((LAST,)),
+            dma((LAST,)),
         ],
-        out_specs=(
-            pl.BlockSpec((step, width), lambda i: (i, 0)),
-            pl.BlockSpec((1, rows), lambda i: (0, 0)),
-        ),
+        compiler_params=pltpu.CompilerParams(vmem_limit_bytes=60 * 2**20),
     )(tok, bent, adjoint, sc)
     return theta, score.reshape(rows)
 

time: 63.1 us -> 60.2 us (0.954)
  Pallas kernels: 62.1 us -> 59.4 us
    pallas_call x1, Pallas kernels: 10.4 us -> 8.89 us  [shards(): pl.pallas_call(last_kernel, out_shape=(jax.ShapeDtypeStruct((D, width), f...]
    pallas_call x1, Pallas kernels: 51.7 us -> 50.5 us  [shards(): pl.pallas_call(functools.partial(main_kernel, n, wide), out_shape=(jax.Sh...]
where the time goes in v2:
time: 60.2 us; the launch traced here: 60 us
  Pallas kernels  59.4 us (99%)
  between operations  0.64 us (1%)
    pallas_call x1, Pallas kernels, shards(): pl.pallas_call(functools.partial(main_kernel, n, wide), out_shape=(jax.Sh...  50.5 us
    pallas_call x1, Pallas kernels, shards(): pl.pallas_call(last_kernel, out_shape=(jax.ShapeDtypeStruct((D, width), f...  8.89 us

profile of v2, /device:TPU:0, one launch (start us, length us, event | category | flops | bytes accessed | tf_op | source)
XLA Modules:
  0.0 60.0 jit_solution(347368088029990059)
XLA Ops:
  0.6 50.5 %shard_map.86 = (bf16[256,4096]{1,0:T(8,128)(2,1)}, bf16[256,512]{1,0:T(8,128)(2,1)}, f32[1,128]{1,0:T(1,128)}) custom-call(bf16[16,4096]{1,0:T(8,128)(2,1)} %x_ref.1, bf16[256,512]{1,0:T(8,128)(2,1)} %cot_ref.1, f32[1,256]{1,0:T(1,128)} %bitcast.2, bf16[4096,512]{1,0:T(8,128)(2,1)} %w_hbm.1, bf16[4096,512]{1,0:T(8,128)(2,1)} %one_hbm.1, ...), custom_call_target="tpu_custom_call" | custom-call | tf_op jit(solution)/shard_map/pallas_call | solution.py:362
  51.1 8.9 %shard_map.87 = (f32[4096,512]{1,0:T(8,128)}, f32[1,16]{1,0:T(1,128)}) custom-call(bf16[256,4096]{1,0:T(8,128)(2,1)} %get-tuple-element.7.tok_hbm, bf16[256,512]{1,0:T(8,128)(2,1)} %get-tuple-element.8.bent_ref, f32[4096,512]{1,0:T(8,128)} %adj_hbm.3, f32[1,128]{1,0:T(1,128)} %get-tuple-element.9.sc_ref), custom_call_target="tpu_custom_call" | custom-call | tf_op jit(solution)/shard_map/pallas_call | solution.py:402

commit v3 on v2

--- a/solution.py
+++ b/solution.py
@@ -79,19 +79,25 @@
             device_id_type=MESH,
         )
 
+    def direct(dev, h):
+        return pltpu.make_async_remote_copy(
+            src_ref=x_ref.at[:, pl.ds(h * cols, cols)],
+            dst_ref=slab(me, h),
+            send_sem=gs.at[0, h, dev],
+            recv_sem=gr.at[h, me],
+            device_id={"dp": dev},
+            device_id_type=MESH,
+        )
+
     def arrive(o, h):
         push(3, o, sibling, h).wait_recv()
 
-    more, less = z + 1 < line, z > 0
-
     for h in range(PIECES):
-        @pl.when(more)
-        def _():
-            push(0, me, me + stride, h, x_ref).start()
-
-        @pl.when(less)
-        def _():
-            push(1, me, me - stride, h, x_ref).start()
+        for k in range(1, line):
+            for way in (-1, 1):
+                @pl.when((z + way * k >= 0) & (z + way * k < line))
+                def _():
+                    direct(me + way * k * stride, h).start()
 
         if wide == 2:
             push(2, me, across, h, x_ref).start()
@@ -110,16 +116,12 @@
 
     for k in range(1, line):
         for h in range(PIECES):
-            for way, kind, onward in ((-1, 0, more), (1, 1, less)):
+            for way in (-1, 1):
                 o = me + way * k * stride
 
                 @pl.when((z + way * k >= 0) & (z + way * k < line))
                 def _():
                     arrive(o, h)
-
-                    @pl.when(onward)
-                    def _():
-                        push(kind, o, me - way * stride, h).start()
 
                     if wide == 2:
                         push(2, o, across, h).start()
@@ -300,13 +302,9 @@
     def sent_line(i, _):
         o = (i * wide + y) * 2 + core
         for h in range(PIECES):
-            @pl.when((i <= z) & more)
+            @pl.when(i != z)
             def _():
-                push(0, o, me + stride, h).wait_send()
-
-            @pl.when((i >= z) & less)
-            def _():
-                push(1, o, me - stride, h).wait_send()
+                direct(o, h).wait_send()
 
             if wide == 2:
                 push(2, o, across, h).wait_send()

time: 60.2 us -> 63.5 us (1.055)
  Pallas kernels: 59.4 us -> 62.7 us
    pallas_call x1, Pallas kernels: 50.5 us -> 53.8 us  [shards(): pl.pallas_call(functools.partial(main_kernel, n, wide), out_shape=(jax.Sh...]
where the time goes in v3:
time: 63.5 us; the launch traced here: 63.3 us
  Pallas kernels  62.7 us (99%)
  between operations  0.64 us (1%)
    pallas_call x1, Pallas kernels, shards(): pl.pallas_call(functools.partial(main_kernel, n, wide), out_shape=(jax.Sh...  53.8 us
    pallas_call x1, Pallas kernels, shards(): pl.pallas_call(last_kernel, out_shape=(jax.ShapeDtypeStruct((D, width), f...  8.89 us

profile of v3, /device:TPU:0, one launch (start us, length us, event | category | flops | bytes accessed | tf_op | source)
XLA Modules:
  0.0 63.3 jit_solution(6648625144187426590)
XLA Ops:
  0.6 53.8 %shard_map.86 = (bf16[256,4096]{1,0:T(8,128)(2,1)}, bf16[256,512]{1,0:T(8,128)(2,1)}, f32[1,128]{1,0:T(1,128)}) custom-call(bf16[16,4096]{1,0:T(8,128)(2,1)} %x_ref.1, bf16[256,512]{1,0:T(8,128)(2,1)} %cot_ref.1, f32[1,256]{1,0:T(1,128)} %bitcast.2, bf16[4096,512]{1,0:T(8,128)(2,1)} %w_hbm.1, bf16[4096,512]{1,0:T(8,128)(2,1)} %one_hbm.1, ...), custom_call_target="tpu_custom_call" | custom-call | tf_op jit(solution)/shard_map/pallas_call | solution.py:360
  54.4 8.9 %shard_map.87 = (f32[4096,512]{1,0:T(8,128)}, f32[1,16]{1,0:T(1,128)}) custom-call(bf16[256,4096]{1,0:T(8,128)(2,1)} %get-tuple-element.7.tok_hbm, bf16[256,512]{1,0:T(8,128)(2,1)} %get-tuple-element.8.bent_ref, f32[4096,512]{1,0:T(8,128)} %adj_hbm.3, f32[1,128]{1,0:T(1,128)} %get-tuple-element.9.sc_ref), custom_call_target="tpu_custom_call" | custom-call | tf_op jit(solution)/shard_map/pallas_call | solution.py:400
